TPU v7x, 512 devices: a whole 4x4x16 slice. The times are simulated.
512 devices in a mesh: row: 32 (over z_hi, x, core), col: 16 (over y, z_lo).
Axes of the slice: x: 4, y: 4, z: 16 (z_hi: 4, z_lo: 4; z = z_hi * 4 + z_lo), core: 2. Of those that a mesh axis runs over, the one named last changes fastest.
Arguments:
- adjoint: bfloat16 [3, 128, 256, 512], P(None, 'col', 'row'), may hold values from -6 to 6
- velocity: bfloat16 [3, 128, 256, 512], P(None, 'col', 'row'), may hold values from -6 to 6
- control: bfloat16 [256, 512], P('row'), may hold values from -6 to 6
- deriv_x: bfloat16 [2, 512, 512], replicated, may hold values from -0.25 to 0.25
- deriv_y: bfloat16 [2, 256, 256], replicated, may hold values from -0.375 to 0.375
- deriv_z: bfloat16 [2, 128, 128], replicated, may hold values from -0.5 to 0.5
Outputs:
- adjoint_rate: bfloat16 [3, 128, 256, 512], P(None, 'col', 'row')
- control_grad: float32 [256, 512], P('row')
All inputs are finite; a program needn't handle non-finite values.
Results may differ from a plain program's by a relative error of at most 0.009.
Values may be sent and summed in bfloat16 or wider, within the bound.
A program may use at most 64 MiB of HBM per device.

v0:
```python
import jax
import jax.numpy as jnp
from jax import lax
from jax.sharding import PartitionSpec as P


def directional(adjoint_in, velocity_in, matrices, component, grid_dim):
    letters = "abcd"
    source = letters[:grid_dim] + "p" + letters[grid_dim + 1 :]
    target = "m" + letters[:grid_dim] + "q" + letters[grid_dim + 1 :]
    stacked = jnp.einsum(
        source + ",mpq->" + target, adjoint_in, matrices, preferred_element_type=jnp.float32
    )
    deriv_term = stacked[0]
    visc_term = stacked[1]
    speeds = velocity_in.astype(jnp.float32)
    summed = visc_term - speeds[component] * deriv_term
    summed = summed.at[component].add(-jnp.sum(speeds * deriv_term, axis=0))
    return summed.astype(jnp.bfloat16)


def on_device(adjoint, velocity, control, deriv_x, deriv_y, deriv_z):
    part_x = directional(adjoint, velocity, deriv_x, 0, 3)
    span_local = jnp.sum(adjoint[0].astype(jnp.float32) * velocity[0].astype(jnp.float32), axis=0)
    control_grad = lax.psum(span_local, "col")
    normal_adj, normal_vel = (
        lax.all_to_all(adjoint, "row", split_axis=3, concat_axis=2, tiled=True),
        lax.all_to_all(velocity, "row", split_axis=3, concat_axis=2, tiled=True),
    )
    part_y = directional(normal_adj, normal_vel, deriv_y, 1, 2)
    span_part = directional(
        lax.all_to_all(normal_adj, "col", split_axis=2, concat_axis=1, tiled=True),
        lax.all_to_all(normal_vel, "col", split_axis=2, concat_axis=1, tiled=True),
        deriv_z,
        2,
        1,
    )
    back_span = lax.all_to_all(span_part, "col", split_axis=1, concat_axis=2, tiled=True)
    side_normal = (part_y.astype(jnp.float32) + back_span.astype(jnp.float32)).astype(jnp.bfloat16)
    side_sum = lax.all_to_all(side_normal, "row", split_axis=2, concat_axis=3, tiled=True)
    summed = part_x.astype(jnp.float32) + side_sum.astype(jnp.float32)
    forcing = control.astype(jnp.float32)[None] * adjoint[0].astype(jnp.float32)
    summed = summed.at[0].add(forcing)
    return (summed.astype(jnp.bfloat16), control_grad)


def solution(mesh):
    in_specs = (
        P(None, "col", "row", None),
        P(None, "col", "row", None),
        P("row", None),
        P(),
        P(),
        P(),
    )
    out_specs = (P(None, "col", "row", None), P("row", None))
    return jax.shard_map(
        on_device, mesh=mesh, in_specs=in_specs, out_specs=out_specs, check_vma=False
    )
```

profile of v0, /device:TPU:4, one launch (start us, length us, event | category | flops | bytes accessed | tf_op | source)
XLA Modules:
  0.0 268.3 jit_solution(13649834393603836144)
XLA Ops:
  0.6 4.4 %copy.52 = bf16[3,8,8,512]{2,1,0,3:T(8,128)(2,1)} copy(bf16[3,8,8,512]{3,2,1,0:T(8,128)(2,1)} %param.15) | data formatting | bytes 393216 | tf_op args[1]
  5.0 5.6 %reshape.186 = bf16[32,2,1536]{2,1,0:T(2,128)(2,1)} reshape(bf16[512,3,8,8]{3,2,1,0:T(8,128)(2,1)} %bitcast.130) | data formatting | bytes 393216
  10.7 18.2 %all-to-all-start.1 = ((bf16[32,2,1536]{2,1,0:T(2,128)(2,1)}), bf16[32,2,1536]{2,1,0:T(2,128)(2,1)S(1)}, u32[]{:S(2)}, u32[]{:S(2)}) async-start(bf16[32,2,1536]{2,1,0:T(2,128)(2,1)} %reshape.186), calls=%async_computation.1 | async-start | bytes 393216 | tf_op jit(solution)/shard_map/all_to_all | solution.py:28
  28.9 3.5 %copy.48 = bf16[3,8,8,512]{2,1,0,3:T(8,128)(2,1)} copy(bf16[3,8,8,512]{3,2,1,0:T(8,128)(2,1)S(1)} %copy-done.2) | data formatting | bytes 393216 | tf_op args[0]
  32.4 5.6 %reshape.182 = bf16[32,2,1536]{2,1,0:T(2,128)(2,1)} reshape(bf16[512,3,8,8]{3,2,1,0:T(8,128)(2,1)} %bitcast.131) | data formatting | bytes 393216
  38.0 8.4 %all-to-all-done.1 = bf16[32,2,1536]{2,1,0:T(2,128)(2,1)S(1)} async-done(((bf16[32,2,1536]{2,1,0:T(2,128)(2,1)}), bf16[32,2,1536]{2,1,0:T(2,128)(2,1)S(1)}, u32[]{:S(2)}, u32[]{:S(2)}) %all-to-all-start.1) | async-done | bytes 196640 | tf_op jit(solution)/shard_map/all_to_all | solution.py:28
  46.4 7.2 %all-to-all-start = ((bf16[32,2,1536]{2,1,0:T(2,128)(2,1)}), bf16[32,2,1536]{2,1,0:T(2,128)(2,1)S(1)}, u32[]{:S(2)}, u32[]{:S(2)}) async-start(bf16[32,2,1536]{2,1,0:T(2,128)(2,1)} %reshape.182), calls=%async_computation | async-start | bytes 393216 | tf_op jit(solution)/shard_map/all_to_all | solution.py:27
  53.6 4.8 %reshape.187 = bf16[512,3,8,8]{3,2,1,0:T(8,128)(2,1)} reshape(bf16[32,2,1536]{2,1,0:T(2,128)(2,1)S(1)} %all-to-all-done.1) | data formatting | bytes 393216
  58.4 4.0 %copy.80 = bf16[3,8,32,8,16]{4,1,0,3,2:T(8,128)(2,1)S(1)} copy(bf16[3,8,32,8,16]{3,1,0,4,2:T(8,128)(2,1)} %bitcast.122) | data formatting | bytes 393216 | tf_op jit(solution)/shard_map/all_to_all | solution.py:28
  64.7 6.3 %all-to-all-done = bf16[32,2,1536]{2,1,0:T(2,128)(2,1)S(1)} async-done(((bf16[32,2,1536]{2,1,0:T(2,128)(2,1)}), bf16[32,2,1536]{2,1,0:T(2,128)(2,1)S(1)}, u32[]{:S(2)}, u32[]{:S(2)}) %all-to-all-start) | async-done | bytes 196640 | tf_op jit(solution)/shard_map/all_to_all | solution.py:27
  71.0 7.4 %all-to-all-start.3 = ((bf16[16,2,3072]{2,1,0:T(2,128)(2,1)}), bf16[16,2,3072]{2,1,0:T(2,128)(2,1)S(1)}, u32[]{:S(2)}, u32[]{:S(2)}) async-start(bf16[16,2,3072]{2,1,0:T(2,128)(2,1)} %reshape.188), calls=%async_computation.3 | async-start | bytes 393216 | tf_op jit(solution)/shard_map/all_to_all | solution.py:33
  78.4 4.8 %reshape.183 = bf16[512,3,8,8]{3,2,1,0:T(8,128)(2,1)} reshape(bf16[32,2,1536]{2,1,0:T(2,128)(2,1)S(1)} %all-to-all-done) | data formatting | bytes 393216
  83.2 4.0 %copy.79 = bf16[3,8,32,8,16]{4,1,0,3,2:T(8,128)(2,1)S(1)} copy(bf16[3,8,32,8,16]{3,1,0,4,2:T(8,128)(2,1)} %bitcast.124) | data formatting | bytes 393216 | tf_op jit(solution)/shard_map/all_to_all | solution.py:27
  89.5 7.5 %all-to-all-start.2 = ((bf16[16,2,3072]{2,1,0:T(2,128)(2,1)}), bf16[16,2,3072]{2,1,0:T(2,128)(2,1)S(1)}, u32[]{:S(2)}, u32[]{:S(2)}) async-start(bf16[16,2,3072]{2,1,0:T(2,128)(2,1)} %reshape.184), calls=%async_computation.2 | async-start | bytes 393216 | tf_op jit(solution)/shard_map/all_to_all | solution.py:32
  97.1 4.8 %copy.50 = bf16[3,8,32,8,16]{4,3,2,1,0:T(8,128)(2,1)} copy(bf16[3,8,32,8,16]{3,1,0,4,2:T(8,128)(2,1)} %bitcast.125) | data formatting | bytes 393216 | tf_op jit(solution)/shard_map/all_to_all | solution.py:27
  119.8 7.6 %all-to-all-start.4 = ((bf16[16,2,3072]{2,1,0:T(2,128)(2,1)}), bf16[16,2,3072]{2,1,0:T(2,128)(2,1)}, u32[]{:S(2)}, u32[]{:S(2)}) async-start(bf16[16,2,3072]{2,1,0:T(2,128)(2,1)} %reshape.190), calls=%async_computation.4 | async-start | bytes 393216 | tf_op jit(solution)/shard_map/all_to_all | solution.py:38
  127.4 2.9 %fusion.2 = f32[2,3,8,256,16]{3,4,2,1,0:T(8,128)} fusion(bf16[3,8,32,8,16]{4,3,2,1,0:T(8,128)(2,1)} %copy.50, bf16[2,256,256]{2,1,0:T(8,128)(2,1)S(1)} %copy-done.6), kind=kOutput, calls=%fused_computation.3 | convolution fusion | flops 100663296 | bytes 1245184 | tf_op jit(solution)/shard_map/abpd,mpq->mabqd/dot_general | solution.py:11
  130.3 3.9 %copy.54 = bf16[3,8,32,8,16]{4,3,2,1,0:T(8,128)(2,1)S(1)} copy(bf16[3,8,32,8,16]{3,1,0,4,2:T(8,128)(2,1)} %bitcast.123) | data formatting | bytes 393216 | tf_op jit(solution)/shard_map/all_to_all | solution.py:28
  140.8 3.7 %copy.65 = f32[3,8,16,16,16]{3,2,4,1,0:T(8,128)} copy(f32[3,8,16,16,16]{4,3,1,2,0:T(8,128)} %convert_bitcast_fusion) | data formatting | bytes 786432 | tf_op jit(solution)/shard_map/convert_element_type | solution.py:39
  150.7 6.8 %all-to-all-start.5 = ((bf16[32,2,1536]{2,1,0:T(2,128)(2,1)}), bf16[32,2,1536]{2,1,0:T(2,128)(2,1)S(1)}, u32[]{:S(2)}, u32[]{:S(2)}) async-start(bf16[32,2,1536]{2,1,0:T(2,128)(2,1)} %reshape.192), calls=%async_computation.5 | async-start | bytes 393216 | tf_op jit(solution)/shard_map/all_to_all | solution.py:40
  158.1 19.1 %all-to-all-done.5 = bf16[32,2,1536]{2,1,0:T(2,128)(2,1)S(1)} async-done(((bf16[32,2,1536]{2,1,0:T(2,128)(2,1)}), bf16[32,2,1536]{2,1,0:T(2,128)(2,1)S(1)}, u32[]{:S(2)}, u32[]{:S(2)}) %all-to-all-start.5) | async-done | bytes 196640 | tf_op jit(solution)/shard_map/all_to_all | solution.py:40
  181.2 4.1 %copy.69 = f32[3,8,8,32,16]{4,3,2,1,0:T(8,128)} copy(f32[3,8,8,32,16]{4,2,3,1,0:T(8,128)} %bitcast.129) | data formatting | bytes 786432 | tf_op jit(solution)/shard_map/convert_element_type | solution.py:41
  185.3 3.6 %reshape.172 = f32[3,8,8,512]{3,2,1,0:T(8,128)S(1)} reshape(f32[3,8,8,32,16]{4,3,2,1,0:T(8,128)} %copy.69) | data formatting | bytes 786432 | tf_op jit(solution)/shard_map/convert_element_type | solution.py:41
  189.9 77.7 %psum.7 = f32[8,512]{1,0:T(8,128)} all-reduce(f32[8,512]{1,0:T(8,128)S(1)} %get-tuple-element.56), channel_id=1, replica_groups=mesh['row'=32,'col'=16] {'col'}, use_global_device_ids=true, to_apply=%region_4.0 | all-reduce | flops 4096 | bytes 32768 | tf_op jit(solution)/shard_map/psum | solution.py:25
  (58 shorter events, 41.4 us)
Async XLA Ops:
  0.6 156.9 %copy-start = (bf16[2,512,512]{2,1,0:T(8,128)(2,1)S(1)}, bf16[2,512,512]{2,1,0:T(8,128)(2,1)}, u32[]{:S(2)}) copy-start(bf16[2,512,512]{2,1,0:T(8,128)(2,1)} %param.17) | copy-start | bytes 3145732
  5.0 23.9 %copy-start.2 = (bf16[3,8,8,512]{3,2,1,0:T(8,128)(2,1)S(1)}, bf16[3,8,8,512]{3,2,1,0:T(8,128)(2,1)}, u32[]{:S(2)}) copy-start(bf16[3,8,8,512]{3,2,1,0:T(8,128)(2,1)} %param.14) | copy-start | bytes 589828
  10.7 35.7 %all-to-all-start.1 = ((bf16[32,2,1536]{2,1,0:T(2,128)(2,1)}), bf16[32,2,1536]{2,1,0:T(2,128)(2,1)S(1)}, u32[]{:S(2)}, u32[]{:S(2)}) async-start(bf16[32,2,1536]{2,1,0:T(2,128)(2,1)} %reshape.186), calls=%async_computation.1 | async-start | bytes 393216 | tf_op jit(solution)/shard_map/all_to_all | solution.py:28
  46.4 24.6 %all-to-all-start = ((bf16[32,2,1536]{2,1,0:T(2,128)(2,1)}), bf16[32,2,1536]{2,1,0:T(2,128)(2,1)S(1)}, u32[]{:S(2)}, u32[]{:S(2)}) async-start(bf16[32,2,1536]{2,1,0:T(2,128)(2,1)} %reshape.182), calls=%async_computation | async-start | bytes 393216 | tf_op jit(solution)/shard_map/all_to_all | solution.py:27
  71.0 18.5 %all-to-all-start.3 = ((bf16[16,2,3072]{2,1,0:T(2,128)(2,1)}), bf16[16,2,3072]{2,1,0:T(2,128)(2,1)S(1)}, u32[]{:S(2)}, u32[]{:S(2)}) async-start(bf16[16,2,3072]{2,1,0:T(2,128)(2,1)} %reshape.188), calls=%async_computation.3 | async-start | bytes 393216 | tf_op jit(solution)/shard_map/all_to_all | solution.py:33
  87.2 9.9 %copy-start.1 = (bf16[3,8,8,512]{3,2,1,0:T(8,128)(2,1)S(1)}, bf16[3,8,8,512]{3,2,1,0:T(8,128)(2,1)}, u32[]{:S(2)}) copy-start(bf16[3,8,8,512]{3,2,1,0:T(8,128)(2,1)} %param.15) | copy-start | bytes 589828
  87.2 9.9 %copy-start.5 = (bf16[8,512]{1,0:T(8,128)(2,1)S(1)}, bf16[8,512]{1,0:T(8,128)(2,1)}, u32[]{:S(2)}) copy-start(bf16[8,512]{1,0:T(8,128)(2,1)} %param.16) | copy-start | bytes 24580
  89.5 17.8 %all-to-all-start.2 = ((bf16[16,2,3072]{2,1,0:T(2,128)(2,1)}), bf16[16,2,3072]{2,1,0:T(2,128)(2,1)S(1)}, u32[]{:S(2)}, u32[]{:S(2)}) async-start(bf16[16,2,3072]{2,1,0:T(2,128)(2,1)} %reshape.184), calls=%async_computation.2 | async-start | bytes 393216 | tf_op jit(solution)/shard_map/all_to_all | solution.py:32
  114.2 1.8 copy-start.4
  116.4 11.0 %copy-start.6 = (bf16[2,256,256]{2,1,0:T(8,128)(2,1)S(1)}, bf16[2,256,256]{2,1,0:T(8,128)(2,1)}, u32[]{:S(2)}) copy-start(bf16[2,256,256]{2,1,0:T(8,128)(2,1)} %param.18) | copy-start | bytes 786436
  119.8 16.3 %all-to-all-start.4 = ((bf16[16,2,3072]{2,1,0:T(2,128)(2,1)}), bf16[16,2,3072]{2,1,0:T(2,128)(2,1)}, u32[]{:S(2)}, u32[]{:S(2)}) async-start(bf16[16,2,3072]{2,1,0:T(2,128)(2,1)} %reshape.190), calls=%async_computation.4 | async-start | bytes 393216 | tf_op jit(solution)/shard_map/all_to_all | solution.py:38
  147.4 10.1 %copy-start.3 = (bf16[3,8,8,512]{3,2,1,0:T(8,128)(2,1)S(1)}, bf16[3,8,8,512]{3,2,1,0:T(8,128)(2,1)}, u32[]{:S(2)}) copy-start(bf16[3,8,8,512]{3,2,1,0:T(8,128)(2,1)} %param.14) | copy-start | bytes 589828
  150.7 26.5 %all-to-all-start.5 = ((bf16[32,2,1536]{2,1,0:T(2,128)(2,1)}), bf16[32,2,1536]{2,1,0:T(2,128)(2,1)S(1)}, u32[]{:S(2)}, u32[]{:S(2)}) async-start(bf16[32,2,1536]{2,1,0:T(2,128)(2,1)} %reshape.192), calls=%async_computation.5 | async-start | bytes 393216 | tf_op jit(solution)/shard_map/all_to_all | solution.py:40
where the time goes:
time: 270 us; the launch traced here: 268 us
  local copies, waits for them, and re-layouts  92.1 us (34%)
  blocking collectives  77.7 us (29%)
  starting transfers between devices  54.7 us (20%)
  waiting for transfers between devices  33.8 us (13%)
  other arithmetic  5.43 us (2%)
  matrix products  3.54 us (1%)
    psum x1, blocking collectives, on_device(): control_grad = lax.psum(span_local, 'col')  77.7 us
    unnamed x28, local copies, waits for them, and re-layouts  43.8 us
    all_to_all x1, waiting for transfers between devices, on_device(): lax.all_to_all(side_normal, 'row', split_axis=2, concat_axis=3, tiled=True)  19.1 us
    all_to_all x1, starting transfers between devices, on_device(): lax.all_to_all(velocity, 'row', split_axis=3, concat_axis=2, tiled=True)  18.2 us
    convert_element_type x3, local copies, waits for them, and re-layouts, on_device(): summed = part_x.astype(jnp.float32) + side_sum.astype(jnp.float32)  9.7 us
    all_to_all x2, local copies, waits for them, and re-layouts, on_device(): lax.all_to_all(adjoint, 'row', split_axis=3, concat_axis=2, tiled=True)  8.76 us
    all_to_all x3, local copies, waits for them, and re-layouts, on_device(): lax.all_to_all(velocity, 'row', split_axis=3, concat_axis=2, tiled=True)  8.46 us
    all_to_all x1, waiting for transfers between devices, on_device(): lax.all_to_all(velocity, 'row', split_axis=3, concat_axis=2, tiled=True)  8.4 us
  transfers between devices with their start and end apart: 6, of which 3 were waited for; matrix products, arithmetic and copies ran while one was open for 19% of the time, Pallas kernels for 0%

commit v1 on v0

v1 whole, which is shorter than its diff:
```python
import functools

import jax
import jax.numpy as jnp
from jax import lax
from jax.experimental import pallas as pl
from jax.experimental.pallas import tpu as pltpu
from jax.sharding import PartitionSpec as P

BF = jnp.bfloat16
F32 = jnp.float32
ROWS = 32
COLS = 16
MESH = pl.DeviceIdType.MESH


def lanes(chunk):
    return pl.ds(pl.multiple_of(chunk * 128, 128), 128)


def remote(src, dst, send_sem, recv_sem, axis, peer):
    return pltpu.make_async_remote_copy(
        src_ref=src,
        dst_ref=dst,
        send_sem=send_sem,
        recv_sem=recv_sem,
        device_id={axis: peer},
        device_id_type=MESH,
    )


def wait_bytes(ref, sem):
    pltpu.make_async_copy(ref, ref, sem).wait()


def tendency(deriv, visc, speeds, d):
    mixed = speeds[0] * deriv[0] + speeds[1] * deriv[1] + speeds[2] * deriv[2]
    out = []
    for k in range(3):
        value = visc[k] - speeds[d] * deriv[k]
        if k == d:
            value = value - mixed
        out.append(value)
    return out


def kernel(
    adj, vel, ctl, dx, dy, dz, out, cg_out,
    adj_t, vel_t, row_adj, row_vel, col_adj, col_vel,
    py, pz, yback, zback, cg_mine, cg_all,
    base, gy, gz, dyt, dzt, send_sems, recv_sems,
):
    row = lax.axis_index("row")
    col = lax.axis_index("col")

    barrier = pltpu.get_barrier_semaphore()

    def greet(axis, me, n):
        def body(i, carry):
            peer = lax.rem(me + i, n)
            pl.semaphore_signal(barrier, inc=1, device_id={axis: peer}, device_id_type=MESH)
            return carry

        lax.fori_loop(1, n, body, 0)

    greet("row", row, ROWS)
    greet("col", col, COLS)

    for src, dst in ((adj, adj_t), (vel, vel_t)):
        for k in range(3):
            dst[:, k] = jnp.swapaxes(src[k].astype(F32), 0, 1).astype(BF)

    pl.semaphore_wait(barrier, ROWS - 1 + COLS - 1)

    def send_all(which, axis, me, n, view, slots):
        def body(i, carry):
            peer = lax.rem(me + i, n)
            remote(
                view(peer), slots.at[me], send_sems.at[which], recv_sems.at[which], axis, peer
            ).start()
            return carry

        lax.fori_loop(1, n, body, 0)
        pltpu.make_async_copy(view(me), slots.at[me], recv_sems.at[which]).start()

    def row_view(ref):
        return lambda r: ref.at[:, r // 4, :, lanes(lax.rem(r, 4))]

    def col_view(ref):
        return lambda c: ref.at[pl.ds(c // 4 * 2, 2), :, :, lanes(lax.rem(c, 4))]

    send_all(0, "row", row, ROWS, row_view(adj), row_adj)
    send_all(1, "row", row, ROWS, row_view(vel), row_vel)
    send_all(2, "col", col, COLS, col_view(adj_t), col_adj)
    send_all(3, "col", col, COLS, col_view(vel_t), col_vel)

    for m in range(2):
        dyt[m * 256 : m * 256 + 256, :] = dy[m].astype(F32).T.astype(BF)
        dzt[m * 128 : m * 128 + 128, :] = dz[m].astype(F32).T.astype(BF)

    flat = adj[...].astype(F32).reshape(192, 512).astype(BF)
    for c in range(2):
        cols = slice(c * 256, c * 256 + 256)
        g0 = jnp.dot(flat, dx[0, :, cols], preferred_element_type=F32)
        g1 = jnp.dot(flat, dx[1, :, cols], preferred_element_type=F32)
        speeds = [vel[k, :, :, cols].astype(F32).reshape(64, 256) for k in range(3)]
        parts = tendency(
            [g0[k * 64 : k * 64 + 64] for k in range(3)],
            [g1[k * 64 : k * 64 + 64] for k in range(3)],
            speeds,
            0,
        )
        for k in range(3):
            value = parts[k].astype(BF).astype(F32).reshape(8, 8, 256)
            if k == 0:
                value = value + ctl[:, cols].astype(F32)[None] * adj[0, :, :, cols].astype(F32)
            base[k, :, :, cols] = value

    wait_bytes(row_adj, recv_sems.at[0])
    lines = jnp.concatenate(
        [row_adj[:, k].astype(F32).reshape(256, 128) for k in range(3)], axis=1
    ).astype(BF)
    gy[...] = jnp.dot(dyt[...], lines, preferred_element_type=F32)
    wait_bytes(row_vel, recv_sems.at[1])
    for c in range(8):
        at = slice(c * 4, c * 4 + 4)
        rows0 = slice(c * 32, c * 32 + 32)
        rows1 = slice(256 + c * 32, 256 + c * 32 + 32)
        parts = tendency(
            [gy[rows0, k * 128 : k * 128 + 128] for k in range(3)],
            [gy[rows1, k * 128 : k * 128 + 128] for k in range(3)],
            [row_vel[at, k].astype(F32).reshape(32, 128) for k in range(3)],
            1,
        )
        for k in range(3):
            py[at, k] = parts[k].reshape(4, 8, 128).astype(BF)
    send_all(4, "row", row, ROWS, lambda r: py.at[r], yback)

    wait_bytes(col_adj, recv_sems.at[2])
    lines = jnp.concatenate(
        [col_adj[:, y, k].astype(F32).reshape(128, 128) for y in range(2) for k in range(3)],
        axis=1,
    ).astype(BF)
    gz[...] = jnp.dot(dzt[...], lines, preferred_element_type=F32)
    wait_bytes(col_vel, recv_sems.at[3])
    for y in range(2):
        cg_mine[y : y + 1, :] = jnp.sum(
            (col_adj[:, y, 0].astype(F32) * col_vel[:, y, 0].astype(F32)).reshape(128, 128),
            axis=0,
            keepdims=True,
        )
    for c in range(4):
        at = slice(c * 4, c * 4 + 4)
        rows0 = slice(c * 32, c * 32 + 32)
        rows1 = slice(128 + c * 32, 128 + c * 32 + 32)
        for y in range(2):
            first = y * 3
            parts = tendency(
                [gz[rows0, (first + k) * 128 : (first + k + 1) * 128] for k in range(3)],
                [gz[rows1, (first + k) * 128 : (first + k + 1) * 128] for k in range(3)],
                [col_vel[at, y, k].astype(F32).reshape(32, 128) for k in range(3)],
                2,
            )
            for k in range(3):
                pz[at, y, k] = parts[k].reshape(4, 8, 128).astype(BF)
    send_all(5, "col", col, COLS, lambda c: pz.at[c], zback)
    send_all(6, "col", col, COLS, lambda c: cg_mine, cg_all)

    wait_bytes(yback, recv_sems.at[4])
    wait_bytes(zback, recv_sems.at[5])
    for x in range(4):
        cols = slice(x * 128, x * 128 + 128)
        for k in range(3):
            span = jnp.stack(
                [zback[(y // 2) * 4 + x, y % 2, k].astype(F32) for y in range(8)], axis=0
            )
            span = jnp.swapaxes(span, 0, 1)
            normal = jnp.stack([yback[z * 4 + x, k].astype(F32) for z in range(8)], axis=0)
            side = (normal + span).astype(BF).astype(F32)
            out[k, :, :, cols] = (base[k, :, :, cols] + side).astype(BF)
    wait_bytes(cg_all, recv_sems.at[6])
    for c in range(COLS):
        yp, x = c // 4, c % 4
        cg_out[yp * 2 : yp * 2 + 2, x * 128 : x * 128 + 128] = cg_all[c]

    for which, slots in enumerate((row_adj, row_vel, col_adj, col_vel, yback, zback, cg_all)):
        wait_bytes(slots.at[pl.ds(0, slots.shape[0] - 1)], send_sems.at[which])


def on_device(adjoint, velocity, control, deriv_x, deriv_y, deriv_z):
    vmem = pl.BlockSpec(memory_space=pltpu.VMEM)
    return pl.pallas_call(
        kernel,
        out_shape=(
            jax.ShapeDtypeStruct((3, 8, 8, 512), BF),
            jax.ShapeDtypeStruct((8, 512), F32),
        ),
        in_specs=[vmem] * 6,
        out_specs=(vmem, vmem),
        scratch_shapes=[
            pltpu.VMEM((8, 3, 8, 512), BF),
            pltpu.VMEM((8, 3, 8, 512), BF),
            pltpu.VMEM((ROWS, 3, 8, 128), BF),
            pltpu.VMEM((ROWS, 3, 8, 128), BF),
            pltpu.VMEM((COLS, 2, 3, 8, 128), BF),
            pltpu.VMEM((COLS, 2, 3, 8, 128), BF),
            pltpu.VMEM((ROWS, 3, 8, 128), BF),
            pltpu.VMEM((COLS, 2, 3, 8, 128), BF),
            pltpu.VMEM((ROWS, 3, 8, 128), BF),
            pltpu.VMEM((COLS, 2, 3, 8, 128), BF),
            pltpu.VMEM((2, 128), F32),
            pltpu.VMEM((COLS, 2, 128), F32),
            pltpu.VMEM((3, 8, 8, 512), F32),
            pltpu.VMEM((512, 384), F32),
            pltpu.VMEM((256, 768), F32),
            pltpu.VMEM((512, 256), BF),
            pltpu.VMEM((256, 128), BF),
            pltpu.SemaphoreType.DMA((7,)),
            pltpu.SemaphoreType.DMA((7,)),
        ],
        compiler_params=pltpu.CompilerParams(collective_id=0, has_side_effects=True),
        name="substep",
    )(adjoint, velocity, control, deriv_x, deriv_y, deriv_z)


def solution(mesh):
    in_specs = (
        P(None, "col", "row", None),
        P(None, "col", "row", None),
        P("row", None),
        P(),
        P(),
        P(),
    )
    out_specs = (P(None, "col", "row", None), P("row", None))
    return jax.shard_map(
        on_device, mesh=mesh, in_specs=in_specs, out_specs=out_specs, check_vma=False
    )
```

time: 270 us -> 66.1 us (0.24)
  the two profiles are of different devices: /device:TPU:4 before, /device:TPU:1 now
where the time goes in v1:
time: 66.1 us; the launch traced here: 65.9 us
  Pallas kernels  63 us (95%)
  local copies, waits for them, and re-layouts  2.23 us (3%)
    pallas_call x1, Pallas kernels, on_device(): pl.pallas_call(kernel, out_shape=(jax.ShapeDtypeStruct((3, 8, 8, 512), BF...  63 us
    unnamed x4, local copies, waits for them, and re-layouts  2.23 us

profile of v1, /device:TPU:1, one launch (start us, length us, event | category | flops | bytes accessed | tf_op | source)
XLA Modules:
  0.0 65.9 jit_solution(2941665783100491621)
XLA Ops:
  0.6 63.0 %substep.1 = (bf16[3,8,8,512]{3,2,1,0:T(8,128)(2,1)}, f32[8,512]{1,0:T(8,128)}) custom-call(bf16[3,8,8,512]{3,2,1,0:T(8,128)(2,1)} %adj.1, bf16[3,8,8,512]{3,2,1,0:T(8,128)(2,1)} %vel.1, bf16[8,512]{1,0:T(8,128)(2,1)} %ctl.1, bf16[2,512,512]{2,1,0:T(8,128)(2,1)} %dx.1, bf16[2,256,256]{2,1,0:T(8,128)(2,1)} %dy.1, bf16[2,128,128]{2,1,0:T(8,128)(2,1)} %dz.1), custom_call_target="tpu_custom_call" | custom-call | tf_op jit(solution)/shard_map/substep/pallas_call | solution.py:192
  63.7 0.0 copy-start
  63.7 1.6 %copy.10 = bf16[3,8,8,512]{3,2,1,0:T(8,128)(2,1)} copy(bf16[3,8,8,512]{3,2,1,0:T(8,128)(2,1)} %get-tuple-element.4) | data formatting | bytes 393216
  65.3 0.0 copy-done
  65.3 0.6 copy.11
Async XLA Ops:
  63.7 1.6 %copy-start = (f32[8,512]{1,0:T(8,128)S(1)}, f32[8,512]{1,0:T(8,128)}, u32[]{:S(2)}) copy-start(f32[8,512]{1,0:T(8,128)} %get-tuple-element.5) | copy-start | bytes 49156

commit v2 on v1

--- a/solution.py
+++ b/solution.py
@@ -45,13 +45,24 @@
 
 
 def kernel(
-    adj, vel, ctl, dx, dy, dz, out, cg_out,
-    adj_t, vel_t, row_adj, row_vel, col_adj, col_vel,
+    adj_in, vel_in, ctl_in, dx_in, dy_in, dz_in, out, cg_out,
+    adj, vel, ctl, dx, dy, dz, relay_adj, relay_vel, relay_py, adj_t, vel_t, row_adj, row_vel, col_adj, col_vel,
     py, pz, yback, zback, cg_mine, cg_all,
-    base, gy, gz, dyt, dzt, send_sems, recv_sems,
+    base, gy, gz, dyt, dzt, send_sems, recv_sems, load_sems, relay_send, relay_recv,
 ):
+    loads = [
+        pltpu.make_async_copy(src, dst, load_sems.at[i])
+        for i, (src, dst) in enumerate(
+            ((adj_in, adj), (vel_in, vel), (ctl_in, ctl), (dx_in, dx), (dy_in, dy), (dz_in, dz))
+        )
+    ]
+    for load in loads:
+        load.start()
     row = lax.axis_index("row")
     col = lax.axis_index("col")
+    part, low = row // 8, lax.rem(row, 8)
+    ahead, behind = lax.rem(part + 1, 4), lax.rem(part + 3, 4)
+    is_relay = lax.rem(row, 2) == 1
 
     barrier = pltpu.get_barrier_semaphore()
 
@@ -66,7 +77,8 @@
     greet("row", row, ROWS)
     greet("col", col, COLS)
 
-    for src, dst in ((adj, adj_t), (vel, vel_t)):
+    for load, src, dst in ((loads[0], adj, adj_t), (loads[1], vel, vel_t)):
+        load.wait()
         for k in range(3):
             dst[:, k] = jnp.swapaxes(src[k].astype(F32), 0, 1).astype(BF)
 
@@ -83,17 +95,66 @@
         lax.fori_loop(1, n, body, 0)
         pltpu.make_async_copy(view(me), slots.at[me], recv_sems.at[which]).start()
 
+    def send_row(which, view, slots, relayed, stop):
+        def send(peer):
+            remote(
+                view(peer), slots.at[row], send_sems.at[which], recv_sems.at[which], "row", peer
+            ).start()
+
+        def opposite(i, carry):
+            place = lax.rem(low + i, 8)
+            peer = lax.rem(part + 2, 4) * 8 + place
+
+            @pl.when(lax.rem(place, 2) == 0)
+            def _():
+                send(peer)
+
+            @pl.when(lax.rem(place, 2) == 1)
+            def _():
+                remote(
+                    view(peer), relayed.at[low], send_sems.at[which], relay_recv.at[stop],
+                    "row", behind * 8 + place,
+                ).start()
+
+            return carry
+
+        def beside(i, carry):
+            place = lax.rem(low + i, 8)
+            send(ahead * 8 + place)
+            send(behind * 8 + place)
+            return carry
+
+        def within(i, carry):
+            send(part * 8 + lax.rem(low + i, 8))
+            return carry
+
+        lax.fori_loop(0, 8, opposite, 0)
+        lax.fori_loop(0, 8, beside, 0)
+        lax.fori_loop(1, 8, within, 0)
+        pltpu.make_async_copy(view(row), slots.at[row], recv_sems.at[which]).start()
+
+    def pass_on(which, slots, relayed, stop):
+        @pl.when(is_relay)
+        def _():
+            wait_bytes(relayed, relay_recv.at[stop])
+            remote(
+                relayed, slots.at[pl.ds(ahead * 8, 8)], relay_send.at[stop], recv_sems.at[which],
+                "row", behind * 8 + low,
+            ).start()
+
     def row_view(ref):
         return lambda r: ref.at[:, r // 4, :, lanes(lax.rem(r, 4))]
 
     def col_view(ref):
         return lambda c: ref.at[pl.ds(c // 4 * 2, 2), :, :, lanes(lax.rem(c, 4))]
 
-    send_all(0, "row", row, ROWS, row_view(adj), row_adj)
-    send_all(1, "row", row, ROWS, row_view(vel), row_vel)
+    send_row(0, row_view(adj), row_adj, relay_adj, 0)
+    send_row(1, row_view(vel), row_vel, relay_vel, 1)
     send_all(2, "col", col, COLS, col_view(adj_t), col_adj)
     send_all(3, "col", col, COLS, col_view(vel_t), col_vel)
 
+    for load in loads[2:]:
+        load.wait()
     for m in range(2):
         dyt[m * 256 : m * 256 + 256, :] = dy[m].astype(F32).T.astype(BF)
         dzt[m * 128 : m * 128 + 128, :] = dz[m].astype(F32).T.astype(BF)
@@ -115,6 +176,9 @@
             if k == 0:
                 value = value + ctl[:, cols].astype(F32)[None] * adj[0, :, :, cols].astype(F32)
             base[k, :, :, cols] = value
+
+    pass_on(0, row_adj, relay_adj, 0)
+    pass_on(1, row_vel, relay_vel, 1)
 
     wait_bytes(row_adj, recv_sems.at[0])
     lines = jnp.concatenate(
@@ -134,7 +198,7 @@
         )
         for k in range(3):
             py[at, k] = parts[k].reshape(4, 8, 128).astype(BF)
-    send_all(4, "row", row, ROWS, lambda r: py.at[r], yback)
+    send_row(4, lambda r: py.at[r], yback, relay_py, 2)
 
     wait_bytes(col_adj, recv_sems.at[2])
     lines = jnp.concatenate(
@@ -166,6 +230,8 @@
     send_all(5, "col", col, COLS, lambda c: pz.at[c], zback)
     send_all(6, "col", col, COLS, lambda c: cg_mine, cg_all)
 
+    pass_on(4, yback, relay_py, 2)
+
     wait_bytes(yback, recv_sems.at[4])
     wait_bytes(zback, recv_sems.at[5])
     for x in range(4):
@@ -186,6 +252,11 @@
     for which, slots in enumerate((row_adj, row_vel, col_adj, col_vel, yback, zback, cg_all)):
         wait_bytes(slots.at[pl.ds(0, slots.shape[0] - 1)], send_sems.at[which])
 
+    @pl.when(is_relay)
+    def _():
+        for stop, relayed in enumerate((relay_adj, relay_vel, relay_py)):
+            wait_bytes(relayed, relay_send.at[stop])
+
 
 def on_device(adjoint, velocity, control, deriv_x, deriv_y, deriv_z):
     vmem = pl.BlockSpec(memory_space=pltpu.VMEM)
@@ -195,9 +266,18 @@
             jax.ShapeDtypeStruct((3, 8, 8, 512), BF),
             jax.ShapeDtypeStruct((8, 512), F32),
         ),
-        in_specs=[vmem] * 6,
+        in_specs=[pl.BlockSpec(memory_space=pl.ANY)] * 6,
         out_specs=(vmem, vmem),
         scratch_shapes=[
+            pltpu.VMEM((3, 8, 8, 512), BF),
+            pltpu.VMEM((3, 8, 8, 512), BF),
+            pltpu.VMEM((8, 512), BF),
+            pltpu.VMEM((2, 512, 512), BF),
+            pltpu.VMEM((2, 256, 256), BF),
+            pltpu.VMEM((2, 128, 128), BF),
+            pltpu.VMEM((8, 3, 8, 128), BF),
+            pltpu.VMEM((8, 3, 8, 128), BF),
+            pltpu.VMEM((8, 3, 8, 128), BF),
             pltpu.VMEM((8, 3, 8, 512), BF),
             pltpu.VMEM((8, 3, 8, 512), BF),
             pltpu.VMEM((ROWS, 3, 8, 128), BF),
@@ -217,6 +297,9 @@
             pltpu.VMEM((256, 128), BF),
             pltpu.SemaphoreType.DMA((7,)),
             pltpu.SemaphoreType.DMA((7,)),
+            pltpu.SemaphoreType.DMA((6,)),
+            pltpu.SemaphoreType.DMA((3,)),
+            pltpu.SemaphoreType.DMA((3,)),
         ],
         compiler_params=pltpu.CompilerParams(collective_id=0, has_side_effects=True),
         name="substep",

time: 66.1 us -> 73.1 us (1.11)
  Pallas kernels: 63 us -> 70 us
    pallas_call x1, Pallas kernels: 63 us -> 70 us  [on_device(): pl.pallas_call(kernel, out_shape=(jax.ShapeDtypeStruct((3, 8, 8, 512), BF...]
where the time goes in v2:
time: 73.1 us; the launch traced here: 72.9 us
  Pallas kernels  70 us (96%)
  local copies, waits for them, and re-layouts  2.23 us (3%)
    pallas_call x1, Pallas kernels, on_device(): pl.pallas_call(kernel, out_shape=(jax.ShapeDtypeStruct((3, 8, 8, 512), BF...  70 us
    unnamed x4, local copies, waits for them, and re-layouts  2.23 us

profile of v2, /device:TPU:1, one launch (start us, length us, event | category | flops | bytes accessed | tf_op | source)
XLA Modules:
  0.0 72.9 jit_solution(17977034634191334403)
XLA Ops:
  0.6 70.0 %substep.1 = (bf16[3,8,8,512]{3,2,1,0:T(8,128)(2,1)}, f32[8,512]{1,0:T(8,128)}) custom-call(bf16[3,8,8,512]{3,2,1,0:T(8,128)(2,1)} %adj_in.1, bf16[3,8,8,512]{3,2,1,0:T(8,128)(2,1)} %vel_in.1, bf16[8,512]{1,0:T(8,128)(2,1)} %ctl_in.1, bf16[2,512,512]{2,1,0:T(8,128)(2,1)} %dx_in.1, bf16[2,256,256]{2,1,0:T(8,128)(2,1)} %dy_in.1, bf16[2,128,128]{2,1,0:T(8,128)(2,1)} %dz_in.1), custom_call_target="tpu_custom_call" | custom-call | tf_op jit(solution)/shard_map/substep/pallas_call | solution.py:263
  70.7 0.0 copy-start
  70.7 1.6 %copy.10 = bf16[3,8,8,512]{3,2,1,0:T(8,128)(2,1)} copy(bf16[3,8,8,512]{3,2,1,0:T(8,128)(2,1)} %get-tuple-element.4) | data formatting | bytes 393216
  72.3 0.0 copy-done
  72.3 0.6 copy.11
Async XLA Ops:
  70.7 1.6 %copy-start = (f32[8,512]{1,0:T(8,128)S(1)}, f32[8,512]{1,0:T(8,128)}, u32[]{:S(2)}) copy-start(f32[8,512]{1,0:T(8,128)} %get-tuple-element.5) | copy-start | bytes 49156

commit v3 on v1

v3 whole, which is shorter than its diff:
```python
import functools

import jax
import jax.numpy as jnp
from jax import lax
from jax.experimental import pallas as pl
from jax.experimental.pallas import tpu as pltpu
from jax.sharding import PartitionSpec as P

BF = jnp.bfloat16
F32 = jnp.float32
MESH = pl.DeviceIdType.MESH


def lanes(chunk):
    return pl.ds(pl.multiple_of(chunk * 128, 128), 128)


def remote(src, dst, send_sem, recv_sem, peer):
    return pltpu.make_async_remote_copy(
        src_ref=src,
        dst_ref=dst,
        send_sem=send_sem,
        recv_sem=recv_sem,
        device_id=peer,
        device_id_type=MESH,
    )


def wait_bytes(ref, sem):
    pltpu.make_async_copy(ref, ref, sem).wait()


def tendency(deriv, visc, speeds, d):
    mixed = speeds[0] * deriv[0] + speeds[1] * deriv[1] + speeds[2] * deriv[2]
    out = []
    for k in range(3):
        value = visc[k] - speeds[d] * deriv[k]
        if k == d:
            value = value - mixed
        out.append(value)
    return out


def kernel(
    adj_in, vel_in, ctl_in, dx_in, dy_in, dz_in, out, cg_out,
    ring_buf, vel, ctl, dx, dy, dz, yin, zin, vy, vz, py, pz, yback, zback,
    cg_part, cg_one, cg_sum, cg_two, cg_mine, cg_all, base, gy, gz, dyt, dzt,
    load_sems, ring_send, ring_recv, send_sems, recv_sems,
):
    row = lax.axis_index("row")
    col = lax.axis_index("col")
    quarter, low = row // 8, lax.rem(row, 8)
    line, step = col // 4, lax.rem(col, 4)
    z = quarter * 4 + step
    adj = ring_buf.at[z]

    loads = [
        pltpu.make_async_copy(src, dst, load_sems.at[i])
        for i, (src, dst) in enumerate(
            ((adj_in, adj), (vel_in, vel), (ctl_in, ctl), (dx_in, dx), (dy_in, dy), (dz_in, dz))
        )
    ]
    for load in loads:
        load.start()

    def at_low(i):
        return (quarter * 8 + lax.rem(low + i, 8), col)

    def at_line(i):
        return (row, lax.rem(line + i, 4) * 4 + step)

    def at_step(i):
        return (row, line * 4 + lax.rem(step + i, 4))

    def at_z(d):
        there = lax.rem(z + d + 16, 16)
        return (there // 4 * 8 + low, line * 4 + lax.rem(there, 4))

    barrier = pltpu.get_barrier_semaphore()
    greeted = [at_z(1), at_z(-1)]
    greeted += [at_low(i) for i in range(1, 8)]
    greeted += [at_line(i) for i in range(1, 4)] + [at_step(i) for i in range(1, 4)]
    for peer in greeted:
        pl.semaphore_signal(barrier, inc=1, device_id=peer, device_id_type=MESH)

    for load in loads:
        load.wait()
    cg_part[...] = jnp.sum(adj[0].astype(F32) * vel[0].astype(F32), axis=0)
    for m in range(2):
        dyt[m * 256 : m * 256 + 256, :] = dy[m].astype(F32).T.astype(BF)
        dzt[m * 128 : m * 128 + 128, :] = dz[m].astype(F32).T
    flat = adj[...].astype(F32).reshape(192, 512).astype(BF)
    for c in range(2):
        cols = slice(c * 256, c * 256 + 256)
        g0 = jnp.dot(flat, dx[0, :, cols], preferred_element_type=F32)
        g1 = jnp.dot(flat, dx[1, :, cols], preferred_element_type=F32)
        parts = tendency(
            [g0[k * 64 : k * 64 + 64] for k in range(3)],
            [g1[k * 64 : k * 64 + 64] for k in range(3)],
            [vel[k, :, :, cols].astype(F32).reshape(64, 256) for k in range(3)],
            0,
        )
        for k in range(3):
            value = parts[k].astype(BF).astype(F32).reshape(8, 8, 256)
            if k == 0:
                value = value + ctl[:, cols].astype(F32)[None] * adj[0, :, :, cols].astype(F32)
            base[k, :, :, cols] = value

    pl.semaphore_wait(barrier, len(greeted))

    def ring(d, s):
        slot = lax.rem(z - d * s + 16, 16)
        if s < 7:
            ref = ring_buf.at[slot]
        else:
            ref = ring_buf.at[slot, :, pl.ds(0 if d > 0 else 4, 4)]
        which = 0 if d > 0 else 1
        return remote(ref, ref, ring_send.at[which], ring_recv.at[which, s], at_z(d))

    def low_sends(which, view, dst, first=0, last=8):
        for i in range(8):
            place = lax.rem(low + i, 8)

            def go(i=i, place=place):
                if i == 0:
                    pltpu.make_async_copy(view(place), dst, recv_sems.at[which]).start()
                else:
                    remote(
                        view(place), dst, send_sems.at[which], recv_sems.at[which], at_low(i)
                    ).start()

            if (first, last) == (0, 8):
                go()
            else:
                pl.when((place >= first) & (place < last))(go)

    def line_sends(which, view, dst):
        for i in range(4):
            place = lax.rem(line + i, 4)
            if i == 0:
                pltpu.make_async_copy(view(place), dst, recv_sems.at[which]).start()
            else:
                remote(
                    view(place), dst, send_sems.at[which], recv_sems.at[which], at_line(i)
                ).start()

    def forward_y(distance, first=0, last=8):
        there = lax.rem(z + distance + 16, 16)
        low_sends(
            0, lambda p: ring_buf.at[there, :, p], yin.at[there // 4 * 8 + low], first, last
        )

    def forward_z(distance):
        there = lax.rem(z + distance + 16, 16)
        line_sends(
            1,
            lambda p: ring_buf.at[there, :, :, :, lanes(p)],
            zin.at[line * 4 + lax.rem(there, 4)],
        )

    ring(1, 0).start()
    ring(-1, 0).start()
    forward_z(0)
    line_sends(3, lambda p: vel.at[:, :, :, lanes(p)], vz.at[line])
    line_sends(6, lambda p: cg_part.at[:, lanes(p)], cg_one.at[line])
    forward_y(0)
    low_sends(2, lambda p: vel.at[:, p], vy.at[low])

    def span_products():
        wait_bytes(zin, recv_sems.at[1])
        wanted = jnp.concatenate(
            [
                dzt[pl.ds(pl.multiple_of(m * 128 + p * 32 + step * 8, 8), 8), :]
                for m in range(2)
                for p in range(4)
            ],
            axis=0,
        ).astype(BF)
        for k in range(3):
            block = jnp.swapaxes(zin[:, k].astype(F32).reshape(128, 8, 128), 0, 1)
            block = jnp.concatenate([block[y] for y in range(8)], axis=1).astype(BF)
            gz[:, k * 1024 : k * 1024 + 1024] = jnp.dot(
                wanted, block, preferred_element_type=F32
            )

    def span_finish(places):
        for p in places:
            def product(m, k):
                at = slice(m * 32 + p * 8, m * 32 + p * 8 + 8)
                tiles = [
                    gz[at, k * 1024 + y * 128 : k * 1024 + y * 128 + 128] for y in range(8)
                ]
                return jnp.swapaxes(jnp.stack(tiles, axis=0), 0, 1)

            parts = tendency(
                [product(0, k) for k in range(3)],
                [product(1, k) for k in range(3)],
                [vz[p, k].astype(F32) for k in range(3)],
                2,
            )
            for k in range(3):
                pz[p, k] = parts[k].astype(BF)

    for s in range(8):
        for d in (1, -1):
            ring(d, s).wait_recv()
            if s < 7:
                ring(d, s + 1).start()
            if s < 3:
                near = step >= s + 1 if d > 0 else step + s + 1 <= 3
                pl.when(near)(functools.partial(forward_z, -d * (s + 1)))
            elif s == 3:
                forward_y(-d * 4)
            elif s == 7:
                forward_y(-d * 8, 0 if d > 0 else 4, 4 if d > 0 else 8)
        if s == 1:
            wait_bytes(cg_one, recv_sems.at[6])
            cg_sum[...] = cg_one[0] + cg_one[1] + cg_one[2] + cg_one[3]
        if s == 2:
            pltpu.make_async_copy(cg_sum, cg_two.at[step], recv_sems.at[7]).start()
            for i in range(1, 4):
                remote(
                    cg_sum, cg_two.at[step], send_sems.at[7], recv_sems.at[7], at_step(i)
                ).start()
        if s == 4:
            span_products()
            wait_bytes(cg_two, recv_sems.at[7])
            cg_mine[...] = cg_two[0] + cg_two[1] + cg_two[2] + cg_two[3]
        if s == 5:
            wait_bytes(vz, recv_sems.at[3])
            span_finish(range(4))
            line_sends(8, lambda p: cg_mine, cg_all.at[line])
        if s == 6:
            line_sends(5, lambda p: pz.at[p], zback.at[line])

    wait_bytes(yin, recv_sems.at[0])
    wait_bytes(vy, recv_sems.at[2])
    wanted = jnp.concatenate(
        [
            dyt[pl.ds(pl.multiple_of(m * 256 + quarter * 64, 64), 64), :]
            for m in range(2)
        ],
        axis=0,
    )
    for k in range(3):
        block = yin[:, k].astype(F32).reshape(256, 512).astype(BF)
        gy[:, k * 512 : k * 512 + 512] = jnp.dot(wanted, block, preferred_element_type=F32)
    for p in range(8):
        for x in range(2):
            cols = slice(x * 256, x * 256 + 256)
            parts = tendency(
                [gy[p * 8 : p * 8 + 8, k * 512 + x * 256 : k * 512 + x * 256 + 256] for k in range(3)],
                [
                    gy[64 + p * 8 : 72 + p * 8, k * 512 + x * 256 : k * 512 + x * 256 + 256]
                    for k in range(3)
                ],
                [vy[p, k, :, cols].astype(F32) for k in range(3)],
                1,
            )
            for k in range(3):
                py[p, k, :, cols] = parts[k].astype(BF)
    low_sends(4, lambda p: py.at[p], yback.at[low])

    wait_bytes(cg_all, recv_sems.at[8])
    for x in range(4):
        cg_out[:, x * 128 : x * 128 + 128] = cg_all[x]
    wait_bytes(zback, recv_sems.at[5])
    wait_bytes(yback, recv_sems.at[4])
    for x in range(4):
        cols = slice(x * 128, x * 128 + 128)
        for k in range(3):
            side = yback[:, k, :, cols].astype(F32) + zback[x, k].astype(F32)
            side = side.astype(BF).astype(F32)
            out[k, :, :, cols] = (base[k, :, :, cols] + side).astype(BF)

    for which in range(2):
        wait_bytes(ring_buf.at[pl.ds(0, 7)], ring_send.at[which])
        wait_bytes(ring_buf.at[0, :, pl.ds(0, 4)], ring_send.at[which])
    sent = (
        yin.at[pl.ds(0, 28)], zin.at[pl.ds(0, 12)], vy.at[pl.ds(0, 7)], vz.at[pl.ds(0, 3)],
        yback.at[pl.ds(0, 7)], zback.at[pl.ds(0, 3)],
        cg_one.at[pl.ds(0, 3)], cg_two.at[pl.ds(0, 3)], cg_all.at[pl.ds(0, 3)],
    )
    for which, ref in enumerate(sent):
        wait_bytes(ref, send_sems.at[which])


def on_device(adjoint, velocity, control, deriv_x, deriv_y, deriv_z):
    vmem = pl.BlockSpec(memory_space=pltpu.VMEM)
    return pl.pallas_call(
        kernel,
        out_shape=(
            jax.ShapeDtypeStruct((3, 8, 8, 512), BF),
            jax.ShapeDtypeStruct((8, 512), F32),
        ),
        in_specs=[pl.BlockSpec(memory_space=pl.ANY)] * 6,
        out_specs=(vmem, vmem),
        scratch_shapes=[
            pltpu.VMEM((16, 3, 8, 8, 512), BF),
            pltpu.VMEM((3, 8, 8, 512), BF),
            pltpu.VMEM((8, 512), BF),
            pltpu.VMEM((2, 512, 512), BF),
            pltpu.VMEM((2, 256, 256), BF),
            pltpu.VMEM((2, 128, 128), BF),
            pltpu.VMEM((32, 3, 8, 512), BF),
            pltpu.VMEM((16, 3, 8, 8, 128), BF),
            pltpu.VMEM((8, 3, 8, 512), BF),
            pltpu.VMEM((4, 3, 8, 8, 128), BF),
            pltpu.VMEM((8, 3, 8, 512), BF),
            pltpu.VMEM((4, 3, 8, 8, 128), BF),
            pltpu.VMEM((8, 3, 8, 512), BF),
            pltpu.VMEM((4, 3, 8, 8, 128), BF),
            pltpu.VMEM((8, 512), F32),
            pltpu.VMEM((4, 8, 128), F32),
            pltpu.VMEM((8, 128), F32),
            pltpu.VMEM((4, 8, 128), F32),
            pltpu.VMEM((8, 128), F32),
            pltpu.VMEM((4, 8, 128), F32),
            pltpu.VMEM((3, 8, 8, 512), F32),
            pltpu.VMEM((128, 1536), F32),
            pltpu.VMEM((64, 3072), F32),
            pltpu.VMEM((512, 256), BF),
            pltpu.VMEM((256, 128), F32),
            pltpu.SemaphoreType.DMA((6,)),
            pltpu.SemaphoreType.DMA((2,)),
            pltpu.SemaphoreType.DMA((2, 8)),
            pltpu.SemaphoreType.DMA((9,)),
            pltpu.SemaphoreType.DMA((9,)),
        ],
        compiler_params=pltpu.CompilerParams(collective_id=0, has_side_effects=True),
        name="substep",
    )(adjoint, velocity, control, deriv_x, deriv_y, deriv_z)


def solution(mesh):
    in_specs = (
        P(None, "col", "row", None),
        P(None, "col", "row", None),
        P("row", None),
        P(),
        P(),
        P(),
    )
    out_specs = (P(None, "col", "row", None), P("row", None))
    return jax.shard_map(
        on_device, mesh=mesh, in_specs=in_specs, out_specs=out_specs, check_vma=False
    )
```

time: 66.1 us -> 72.5 us (1.097)
  Pallas kernels: 63 us -> 69.5 us
    pallas_call x1, Pallas kernels: 63 us -> 69.5 us  [on_device(): pl.pallas_call(kernel, out_shape=(jax.ShapeDtypeStruct((3, 8, 8, 512), BF...]
where the time goes in v3:
time: 72.5 us; the launch traced here: 72.3 us
  Pallas kernels  69.5 us (96%)
  local copies, waits for them, and re-layouts  2.23 us (3%)
    pallas_call x1, Pallas kernels, on_device(): pl.pallas_call(kernel, out_shape=(jax.ShapeDtypeStruct((3, 8, 8, 512), BF...  69.5 us
    unnamed x4, local copies, waits for them, and re-layouts  2.23 us

profile of v3, /device:TPU:1, one launch (start us, length us, event | category | flops | bytes accessed | tf_op | source)
XLA Modules:
  0.0 72.3 jit_solution(17028452226974589517)
XLA Ops:
  0.6 69.5 %substep.1 = (bf16[3,8,8,512]{3,2,1,0:T(8,128)(2,1)}, f32[8,512]{1,0:T(8,128)}) custom-call(bf16[3,8,8,512]{3,2,1,0:T(8,128)(2,1)} %adj_in.1, bf16[3,8,8,512]{3,2,1,0:T(8,128)(2,1)} %vel_in.1, bf16[8,512]{1,0:T(8,128)(2,1)} %ctl_in.1, bf16[2,512,512]{2,1,0:T(8,128)(2,1)} %dx_in.1, bf16[2,256,256]{2,1,0:T(8,128)(2,1)} %dy_in.1, bf16[2,128,128]{2,1,0:T(8,128)(2,1)} %dz_in.1), custom_call_target="tpu_custom_call" | custom-call | tf_op jit(solution)/shard_map/substep/pallas_call | solution.py:291
  70.1 0.0 copy-start
  70.1 1.6 %copy.10 = bf16[3,8,8,512]{3,2,1,0:T(8,128)(2,1)} copy(bf16[3,8,8,512]{3,2,1,0:T(8,128)(2,1)} %get-tuple-element.4) | data formatting | bytes 393216
  71.7 0.0 copy-done
  71.7 0.6 copy.11
Async XLA Ops:
  70.1 1.6 %copy-start = (f32[8,512]{1,0:T(8,128)S(1)}, f32[8,512]{1,0:T(8,128)}, u32[]{:S(2)}) copy-start(f32[8,512]{1,0:T(8,128)} %get-tuple-element.5) | copy-start | bytes 49156

commit v4 on v3

--- a/solution.py
+++ b/solution.py
@@ -109,14 +109,14 @@
 
     pl.semaphore_wait(barrier, len(greeted))
 
-    def ring(d, s):
+    def ring(d, s, k):
         slot = lax.rem(z - d * s + 16, 16)
         if s < 7:
-            ref = ring_buf.at[slot]
+            ref = ring_buf.at[slot, k]
         else:
-            ref = ring_buf.at[slot, :, pl.ds(0 if d > 0 else 4, 4)]
+            ref = ring_buf.at[slot, k, pl.ds(0 if d > 0 else 4, 4)]
         which = 0 if d > 0 else 1
-        return remote(ref, ref, ring_send.at[which], ring_recv.at[which, s], at_z(d))
+        return remote(ref, ref, ring_send.at[which], ring_recv.at[which, s, k], at_z(d))
 
     def low_sends(which, view, dst, first=0, last=8):
         for i in range(8):
@@ -159,8 +159,9 @@
             zin.at[line * 4 + lax.rem(there, 4)],
         )
 
-    ring(1, 0).start()
-    ring(-1, 0).start()
+    for k in range(3):
+        ring(1, 0, k).start()
+        ring(-1, 0, k).start()
     forward_z(0)
     line_sends(3, lambda p: vel.at[:, :, :, lanes(p)], vz.at[line])
     line_sends(6, lambda p: cg_part.at[:, lanes(p)], cg_one.at[line])
@@ -203,10 +204,12 @@
                 pz[p, k] = parts[k].astype(BF)
 
     for s in range(8):
+        for k in range(3):
+            for d in (1, -1):
+                ring(d, s, k).wait_recv()
+                if s < 7:
+                    ring(d, s + 1, k).start()
         for d in (1, -1):
-            ring(d, s).wait_recv()
-            if s < 7:
-                ring(d, s + 1).start()
             if s < 3:
                 near = step >= s + 1 if d > 0 else step + s + 1 <= 3
                 pl.when(near)(functools.partial(forward_z, -d * (s + 1)))
@@ -324,7 +327,7 @@
             pltpu.VMEM((256, 128), F32),
             pltpu.SemaphoreType.DMA((6,)),
             pltpu.SemaphoreType.DMA((2,)),
-            pltpu.SemaphoreType.DMA((2, 8)),
+            pltpu.SemaphoreType.DMA((2, 8, 3)),
             pltpu.SemaphoreType.DMA((9,)),
             pltpu.SemaphoreType.DMA((9,)),
         ],

time: 72.5 us -> 63.1 us (0.87)
  Pallas kernels: 69.5 us -> 60 us
    pallas_call x1, Pallas kernels: 69.5 us -> 60 us  [on_device(): pl.pallas_call(kernel, out_shape=(jax.ShapeDtypeStruct((3, 8, 8, 512), BF...]
where the time goes in v4:
time: 63.1 us; the launch traced here: 62.9 us
  Pallas kernels  60 us (95%)
  local copies, waits for them, and re-layouts  2.23 us (4%)
  between operations  0.65 us (1%)
    pallas_call x1, Pallas kernels, on_device(): pl.pallas_call(kernel, out_shape=(jax.ShapeDtypeStruct((3, 8, 8, 512), BF...  60 us
    unnamed x4, local copies, waits for them, and re-layouts  2.23 us

profile of v4, /device:TPU:1, one launch (start us, length us, event | category | flops | bytes accessed | tf_op | source)
XLA Modules:
  0.0 62.9 jit_solution(4087284198396267947)
XLA Ops:
  0.6 60.0 %substep.1 = (bf16[3,8,8,512]{3,2,1,0:T(8,128)(2,1)}, f32[8,512]{1,0:T(8,128)}) custom-call(bf16[3,8,8,512]{3,2,1,0:T(8,128)(2,1)} %adj_in.1, bf16[3,8,8,512]{3,2,1,0:T(8,128)(2,1)} %vel_in.1, bf16[8,512]{1,0:T(8,128)(2,1)} %ctl_in.1, bf16[2,512,512]{2,1,0:T(8,128)(2,1)} %dx_in.1, bf16[2,256,256]{2,1,0:T(8,128)(2,1)} %dy_in.1, bf16[2,128,128]{2,1,0:T(8,128)(2,1)} %dz_in.1), custom_call_target="tpu_custom_call" | custom-call | tf_op jit(solution)/shard_map/substep/pallas_call | solution.py:294
  60.7 0.0 copy-start
  60.7 1.6 %copy.10 = bf16[3,8,8,512]{3,2,1,0:T(8,128)(2,1)} copy(bf16[3,8,8,512]{3,2,1,0:T(8,128)(2,1)} %get-tuple-element.4) | data formatting | bytes 393216
  62.3 0.0 copy-done
  62.3 0.6 copy.11
Async XLA Ops:
  60.7 1.6 %copy-start = (f32[8,512]{1,0:T(8,128)S(1)}, f32[8,512]{1,0:T(8,128)}, u32[]{:S(2)}) copy-start(f32[8,512]{1,0:T(8,128)} %get-tuple-element.5) | copy-start | bytes 49156

commit v5 on v3

--- a/solution.py
+++ b/solution.py
@@ -84,14 +84,15 @@
     for peer in greeted:
         pl.semaphore_signal(barrier, inc=1, device_id=peer, device_id_type=MESH)
 
-    for load in loads:
-        load.wait()
-    cg_part[...] = jnp.sum(adj[0].astype(F32) * vel[0].astype(F32), axis=0)
-    for m in range(2):
-        dyt[m * 256 : m * 256 + 256, :] = dy[m].astype(F32).T.astype(BF)
-        dzt[m * 128 : m * 128 + 128, :] = dz[m].astype(F32).T
-    flat = adj[...].astype(F32).reshape(192, 512).astype(BF)
-    for c in range(2):
+    loads[0].wait()
+    def prepare():
+        cg_part[...] = jnp.sum(adj[0].astype(F32) * vel[0].astype(F32), axis=0)
+        for m in range(2):
+            dyt[m * 256 : m * 256 + 256, :] = dy[m].astype(F32).T.astype(BF)
+            dzt[m * 128 : m * 128 + 128, :] = dz[m].astype(F32).T
+
+    def stream_part(c):
+        flat = adj[...].astype(F32).reshape(192, 512).astype(BF)
         cols = slice(c * 256, c * 256 + 256)
         g0 = jnp.dot(flat, dx[0, :, cols], preferred_element_type=F32)
         g1 = jnp.dot(flat, dx[1, :, cols], preferred_element_type=F32)
@@ -109,14 +110,14 @@
 
     pl.semaphore_wait(barrier, len(greeted))
 
-    def ring(d, s):
+    def ring(d, s, piece):
         slot = lax.rem(z - d * s + 16, 16)
-        if s < 7:
-            ref = ring_buf.at[slot]
-        else:
-            ref = ring_buf.at[slot, :, pl.ds(0 if d > 0 else 4, 4)]
+        ref = ring_buf.at[slot, piece // 2, pl.ds(piece % 2 * 4, 4)]
         which = 0 if d > 0 else 1
-        return remote(ref, ref, ring_send.at[which], ring_recv.at[which, s], at_z(d))
+        return remote(ref, ref, ring_send.at[which], ring_recv.at[which, s, piece], at_z(d))
+
+    def carried(d, s):
+        return range(6) if s < 4 else range(0 if d > 0 else 1, 6, 2)
 
     def low_sends(which, view, dst, first=0, last=8):
         for i in range(8):
@@ -145,10 +146,15 @@
                     view(place), dst, send_sems.at[which], recv_sems.at[which], at_line(i)
                 ).start()
 
-    def forward_y(distance, first=0, last=8):
+    def forward_y(distance, first=0, last=8, k=None):
         there = lax.rem(z + distance + 16, 16)
+        what = slice(None) if k is None else k
         low_sends(
-            0, lambda p: ring_buf.at[there, :, p], yin.at[there // 4 * 8 + low], first, last
+            0,
+            lambda p: ring_buf.at[there, what, p],
+            yin.at[there // 4 * 8 + low, what],
+            first,
+            last,
         )
 
     def forward_z(distance):
@@ -159,13 +165,16 @@
             zin.at[line * 4 + lax.rem(there, 4)],
         )
 
-    ring(1, 0).start()
-    ring(-1, 0).start()
+    for piece in range(6):
+        ring(1, 0, piece).start()
+        ring(-1, 0, piece).start()
+    for load in loads[1:]:
+        load.wait()
     forward_z(0)
     line_sends(3, lambda p: vel.at[:, :, :, lanes(p)], vz.at[line])
-    line_sends(6, lambda p: cg_part.at[:, lanes(p)], cg_one.at[line])
     forward_y(0)
     low_sends(2, lambda p: vel.at[:, p], vy.at[low])
+    prepare()
 
     def span_products():
         wait_bytes(zin, recv_sems.at[1])
@@ -203,36 +212,45 @@
                 pz[p, k] = parts[k].astype(BF)
 
     for s in range(8):
+        for piece in range(6):
+            for d in (1, -1):
+                if piece in carried(d, s):
+                    ring(d, s, piece).wait_recv()
+                    if s < 7 and piece in carried(d, s + 1):
+                        ring(d, s + 1, piece).start()
+                    if s == 7:
+                        half = piece % 2 * 4
+                        forward_y(-d * 8, half, half + 4, piece // 2)
         for d in (1, -1):
-            ring(d, s).wait_recv()
-            if s < 7:
-                ring(d, s + 1).start()
             if s < 3:
                 near = step >= s + 1 if d > 0 else step + s + 1 <= 3
                 pl.when(near)(functools.partial(forward_z, -d * (s + 1)))
             elif s == 3:
                 forward_y(-d * 4)
-            elif s == 7:
-                forward_y(-d * 8, 0 if d > 0 else 4, 4 if d > 0 else 8)
+        if s == 0:
+            stream_part(0)
+            line_sends(6, lambda p: cg_part.at[:, lanes(p)], cg_one.at[line])
         if s == 1:
+            stream_part(1)
+        if s == 3:
+            span_products()
+            wait_bytes(vz, recv_sems.at[3])
             wait_bytes(cg_one, recv_sems.at[6])
             cg_sum[...] = cg_one[0] + cg_one[1] + cg_one[2] + cg_one[3]
-        if s == 2:
+        if s >= 4:
+            span_finish([s - 4])
+        if s == 4:
             pltpu.make_async_copy(cg_sum, cg_two.at[step], recv_sems.at[7]).start()
             for i in range(1, 4):
                 remote(
                     cg_sum, cg_two.at[step], send_sems.at[7], recv_sems.at[7], at_step(i)
                 ).start()
-        if s == 4:
-            span_products()
+        if s == 6:
             wait_bytes(cg_two, recv_sems.at[7])
             cg_mine[...] = cg_two[0] + cg_two[1] + cg_two[2] + cg_two[3]
-        if s == 5:
-            wait_bytes(vz, recv_sems.at[3])
-            span_finish(range(4))
-            line_sends(8, lambda p: cg_mine, cg_all.at[line])
-        if s == 6:
-            line_sends(5, lambda p: pz.at[p], zback.at[line])
+
+    line_sends(5, lambda p: pz.at[p], zback.at[line])
+    line_sends(8, lambda p: cg_mine, cg_all.at[line])
 
     wait_bytes(yin, recv_sems.at[0])
     wait_bytes(vy, recv_sems.at[2])
@@ -275,8 +293,7 @@
             out[k, :, :, cols] = (base[k, :, :, cols] + side).astype(BF)
 
     for which in range(2):
-        wait_bytes(ring_buf.at[pl.ds(0, 7)], ring_send.at[which])
-        wait_bytes(ring_buf.at[0, :, pl.ds(0, 4)], ring_send.at[which])
+        wait_bytes(ring_buf.at[pl.ds(0, 6)], ring_send.at[which])
     sent = (
         yin.at[pl.ds(0, 28)], zin.at[pl.ds(0, 12)], vy.at[pl.ds(0, 7)], vz.at[pl.ds(0, 3)],
         yback.at[pl.ds(0, 7)], zback.at[pl.ds(0, 3)],
@@ -324,7 +341,7 @@
             pltpu.VMEM((256, 128), F32),
             pltpu.SemaphoreType.DMA((6,)),
             pltpu.SemaphoreType.DMA((2,)),
-            pltpu.SemaphoreType.DMA((2, 8)),
+            pltpu.SemaphoreType.DMA((2, 8, 6)),
             pltpu.SemaphoreType.DMA((9,)),
             pltpu.SemaphoreType.DMA((9,)),
         ],

time: 72.5 us -> 59.7 us (0.82)
  Pallas kernels: 69.5 us -> 56.6 us
    pallas_call x1, Pallas kernels: 69.5 us -> 56.6 us  [on_device(): pl.pallas_call(kernel, out_shape=(jax.ShapeDtypeStruct((3, 8, 8, 512), BF...]
where the time goes in v5:
time: 59.7 us; the launch traced here: 59.5 us
  Pallas kernels  56.6 us (95%)
  local copies, waits for them, and re-layouts  2.23 us (4%)
  between operations  0.65 us (1%)
    pallas_call x1, Pallas kernels, on_device(): pl.pallas_call(kernel, out_shape=(jax.ShapeDtypeStruct((3, 8, 8, 512), BF...  56.6 us
    unnamed x4, local copies, waits for them, and re-layouts  2.23 us

profile of v5, /device:TPU:1, one launch (start us, length us, event | category | flops | bytes accessed | tf_op | source)
XLA Modules:
  0.0 59.5 jit_solution(1272590935394010641)
XLA Ops:
  0.6 56.6 %substep.1 = (bf16[3,8,8,512]{3,2,1,0:T(8,128)(2,1)}, f32[8,512]{1,0:T(8,128)}) custom-call(bf16[3,8,8,512]{3,2,1,0:T(8,128)(2,1)} %adj_in.1, bf16[3,8,8,512]{3,2,1,0:T(8,128)(2,1)} %vel_in.1, bf16[8,512]{1,0:T(8,128)(2,1)} %ctl_in.1, bf16[2,512,512]{2,1,0:T(8,128)(2,1)} %dx_in.1, bf16[2,256,256]{2,1,0:T(8,128)(2,1)} %dy_in.1, bf16[2,128,128]{2,1,0:T(8,128)(2,1)} %dz_in.1), custom_call_target="tpu_custom_call" | custom-call | tf_op jit(solution)/shard_map/substep/pallas_call | solution.py:308
  57.3 0.0 copy-start
  57.3 1.6 %copy.10 = bf16[3,8,8,512]{3,2,1,0:T(8,128)(2,1)} copy(bf16[3,8,8,512]{3,2,1,0:T(8,128)(2,1)} %get-tuple-element.4) | data formatting | bytes 393216
  58.9 0.0 copy-done
  58.9 0.6 %copy.11 = f32[8,512]{1,0:T(8,128)} copy(f32[8,512]{1,0:T(8,128)S(1)} %copy-done) | data formatting | bytes 32768
Async XLA Ops:
  57.3 1.6 %copy-start = (f32[8,512]{1,0:T(8,128)S(1)}, f32[8,512]{1,0:T(8,128)}, u32[]{:S(2)}) copy-start(f32[8,512]{1,0:T(8,128)} %get-tuple-element.5) | copy-start | bytes 49156

commit v6 on v5

--- a/solution.py
+++ b/solution.py
@@ -165,9 +165,10 @@
             zin.at[line * 4 + lax.rem(there, 4)],
         )
 
-    for piece in range(6):
-        ring(1, 0, piece).start()
-        ring(-1, 0, piece).start()
+    order = {1: (0, 2, 4, 1, 3, 5), -1: (1, 3, 5, 0, 2, 4)}
+    for place in range(6):
+        for d in (1, -1):
+            ring(d, 0, order[d][place]).start()
     for load in loads[1:]:
         load.wait()
     forward_z(0)
@@ -212,8 +213,9 @@
                 pz[p, k] = parts[k].astype(BF)
 
     for s in range(8):
-        for piece in range(6):
+        for place in range(6):
             for d in (1, -1):
+                piece = order[d][place]
                 if piece in carried(d, s):
                     ring(d, s, piece).wait_recv()
                     if s < 7 and piece in carried(d, s + 1):
@@ -261,24 +263,25 @@
         ],
         axis=0,
     )
-    for k in range(3):
-        block = yin[:, k].astype(F32).reshape(256, 512).astype(BF)
-        gy[:, k * 512 : k * 512 + 512] = jnp.dot(wanted, block, preferred_element_type=F32)
-    for p in range(8):
-        for x in range(2):
-            cols = slice(x * 256, x * 256 + 256)
-            parts = tendency(
-                [gy[p * 8 : p * 8 + 8, k * 512 + x * 256 : k * 512 + x * 256 + 256] for k in range(3)],
+    for x in range(2):
+        cols = slice(x * 256, x * 256 + 256)
+        for k in range(3):
+            block = yin[:, k, :, cols].astype(F32).reshape(256, 256).astype(BF)
+            gy[:, k * 512 + x * 256 : k * 512 + x * 256 + 256] = jnp.dot(
+                wanted, block, preferred_element_type=F32
+            )
+        for p in range(8):
+            g = [
                 [
-                    gy[64 + p * 8 : 72 + p * 8, k * 512 + x * 256 : k * 512 + x * 256 + 256]
+                    gy[m * 64 + p * 8 : m * 64 + p * 8 + 8, k * 512 + x * 256 : k * 512 + x * 256 + 256]
                     for k in range(3)
-                ],
-                [vy[p, k, :, cols].astype(F32) for k in range(3)],
-                1,
-            )
+                ]
+                for m in range(2)
+            ]
+            parts = tendency(g[0], g[1], [vy[p, k, :, cols].astype(F32) for k in range(3)], 1)
             for k in range(3):
                 py[p, k, :, cols] = parts[k].astype(BF)
-    low_sends(4, lambda p: py.at[p], yback.at[low])
+        low_sends(4, lambda p: py.at[p, :, :, cols], yback.at[low, :, :, cols])
 
     wait_bytes(cg_all, recv_sems.at[8])
     for x in range(4):

time: 59.7 us -> 59.2 us (level)
  no operation moved by 1% of the time
where the time goes in v6:
time: 59.2 us; the launch traced here: 59 us
  Pallas kernels  56.1 us (95%)
  local copies, waits for them, and re-layouts  2.23 us (4%)
  between operations  0.65 us (1%)
    pallas_call x1, Pallas kernels, on_device(): pl.pallas_call(kernel, out_shape=(jax.ShapeDtypeStruct((3, 8, 8, 512), BF...  56.1 us
    unnamed x4, local copies, waits for them, and re-layouts  2.23 us

profile of v6, /device:TPU:1, one launch (start us, length us, event | category | flops | bytes accessed | tf_op | source)
XLA Modules:
  0.0 59.0 jit_solution(2976418207646060917)
XLA Ops:
  0.6 56.1 %substep.1 = (bf16[3,8,8,512]{3,2,1,0:T(8,128)(2,1)}, f32[8,512]{1,0:T(8,128)}) custom-call(bf16[3,8,8,512]{3,2,1,0:T(8,128)(2,1)} %adj_in.1, bf16[3,8,8,512]{3,2,1,0:T(8,128)(2,1)} %vel_in.1, bf16[8,512]{1,0:T(8,128)(2,1)} %ctl_in.1, bf16[2,512,512]{2,1,0:T(8,128)(2,1)} %dx_in.1, bf16[2,256,256]{2,1,0:T(8,128)(2,1)} %dy_in.1, bf16[2,128,128]{2,1,0:T(8,128)(2,1)} %dz_in.1), custom_call_target="tpu_custom_call" | custom-call | tf_op jit(solution)/shard_map/substep/pallas_call | solution.py:311
  56.8 0.0 copy-start
  56.8 1.6 %copy.10 = bf16[3,8,8,512]{3,2,1,0:T(8,128)(2,1)} copy(bf16[3,8,8,512]{3,2,1,0:T(8,128)(2,1)} %get-tuple-element.4) | data formatting | bytes 393216
  58.4 0.0 copy-done
  58.4 0.6 %copy.11 = f32[8,512]{1,0:T(8,128)} copy(f32[8,512]{1,0:T(8,128)S(1)} %copy-done) | data formatting | bytes 32768
Async XLA Ops:
  56.8 1.6 %copy-start = (f32[8,512]{1,0:T(8,128)S(1)}, f32[8,512]{1,0:T(8,128)}, u32[]{:S(2)}) copy-start(f32[8,512]{1,0:T(8,128)} %get-tuple-element.5) | copy-start | bytes 49156
